TPU v7x, 32 devices: a whole 2x2x4 slice. The times are simulated.
32 devices in a mesh: dom: 8 (over z, y), sub: 4 (over x, core).
Axes of the slice: x: 2, y: 2, z: 4, core: 2. Of those that a mesh axis runs over, the one named last changes fastest.
Arguments:
- nodal_values: float32 [512, 8192], P(None, ('dom', 'sub')), may hold values from -6 to 6
- kappa: float32 [512, 8192], P(None, ('dom', 'sub')), may hold values from 0.25 to 4
- levels: int32 [8192], P(('dom', 'sub')), may hold values from 0 to 3
- local_faces: int32 [2, 2048], P(None, ('dom', 'sub')), may hold values from 0 to 511, as said below
- sub_faces: int32 [2, 1024], P(None, ('dom', 'sub')), may hold values from 0 to 511, as said below
- near_faces: int32 [2, 1024], P(None, ('dom', 'sub')), may hold values from 512 to 1023, as said below
- far_faces: int32 [2, 384], P(None, ('dom', 'sub')), may hold values from 1024 to 1535, as said below
- child_faces: int32 [4, 96], P(None, ('dom', 'sub')), may hold values from 1024 to 1279, as said below
- child_peer: int32 [96], P(('dom', 'sub')), may hold values from 0 to 7, as said below
- coarse_faces: int32 [256], P(('dom', 'sub')), may hold values from -1 to 1535, as said below
Outputs:
- applied: float32 [512, 8192], P(None, ('dom', 'sub'))
Inputs may be any that keep to these rules, and one draw needn't show every extreme that they name: `local_faces`: row 0 holds faces f = 1 and row 1 faces f = 0 of distinct elements of the same device; column k of both rows is one shared face. `sub_faces`: row 0 holds faces f = 0, row 1 faces f = 1, of distinct elements; entries toward a missing neighbour are boundary faces. `near_faces`: row 0 holds faces f = 2, row 1 faces f = 3, of distinct elements; entries toward a missing neighbour are boundary faces. `far_faces`: row 0 holds faces f = 4, row 1 faces f = 5, of distinct elements; entries toward a missing partner are boundary faces. `child_faces`: faces f = 4 of distinct elements, distinct from all far faces; row m is the child at subface position (m // 2, m % 2). `child_peer`: A device's 3 groups name distinct dom indices other than its own; in every draw one device per sub index is named by every other dom index. `coarse_faces`: slot p is the face f = 5 that takes the group which the device of dom index p (same sub index) sends here, -1 where it sends none; faces are of distinct elements, distinct from all far faces.
All inputs are finite; a program needn't handle non-finite values.
Results may differ from a plain program's by a relative error of at most 0.0003.
Values sent between devices are 32-bit elements; how exact they have to be, the bound alone decides.
A program may use at most 64 MiB of HBM per device.

v0:
```python
import jax
import jax.numpy as jnp
import numpy as np
from jax import lax
from jax.sharding import PartitionSpec as P

NPTS = 8
FAR = 4
SHIFTS = 3


HIGHEST = lax.Precision.HIGHEST


def from_behind(block, axis, distance):
    devices = range(lax.axis_size(axis))
    route = [(i - distance, i) for i in devices if i - distance in devices]
    return lax.ppermute(block, axis, route)


def extended(cells, sides, width):
    for axis, dim in sides:
        count = lax.axis_size(axis)
        ends = count - 1
        head = lax.slice_in_dim(cells, 0, width, axis=dim)
        tail = lax.slice_in_dim(cells, cells.shape[dim] - width, cells.shape[dim], axis=dim)
        cells = jnp.concatenate(
            [
                lax.ppermute(tail, axis, [(i, (i + 1) % count) for i in range(ends)]),
                cells,
                lax.ppermute(head, axis, [((i + 1) % count, i) for i in range(ends)]),
            ],
            axis=dim,
        )
    return cells


def legendre_table(points, degree):
    table = [np.ones(points.shape), points.copy()]
    for order in range(2, degree + 1):
        table.append(
            ((2 * order - 1) * points * table[order - 1] - (order - 1) * table[order - 2]) / order
        )
    return table


def lobatto_points(degree):
    points = np.cos(np.pi * np.arange(degree + 1) / degree)
    for sweep in range(100):
        table = legendre_table(points, degree)
        points = points - (points * table[degree] - table[degree - 1]) / (
            (degree + 1) * table[degree]
        )
    points = np.sort(points)
    return (points, legendre_table(points, degree)[degree])


def node_tables(count):
    degree = count - 1
    points, legendre = lobatto_points(degree)
    weights = 2.0 / (degree * (degree + 1) * legendre**2)
    spread = points[:, None] - points[None, :] + np.eye(count)
    derivative = legendre[:, None] / (legendre[None, :] * spread) * (1.0 - np.eye(count))
    derivative[0, 0] = -degree * (degree + 1) / 4.0
    derivative[degree, degree] = degree * (degree + 1) / 4.0
    halves = []
    for side in range(2):
        target = (points + 2.0 * side - 1.0) / 2.0
        matrix = np.ones((count, count))
        for column in range(count):
            for other in range(count):
                if other != column:
                    matrix[:, column] = (
                        matrix[:, column]
                        * (target - points[other])
                        / (points[column] - points[other])
                    )
        halves.append(matrix)
    return (points, weights, derivative, np.stack(halves))


def stiffness(values, coeffs, level):
    points, weights, derivative, halves = node_tables(NPTS)
    deriv = jnp.asarray(derivative, jnp.float32)
    elems = values.shape[1]
    cube = values.reshape(NPTS, NPTS, NPTS, elems)
    weight_cube = jnp.asarray(
        weights[:, None, None] * weights[None, :, None] * weights[None, None, :], jnp.float32
    )
    scale = jnp.power(jnp.float32(0.5), level.astype(jnp.float32))
    geometry = (
        coeffs.reshape(NPTS, NPTS, NPTS, elems)
        * weight_cube[:, :, :, None]
        * scale[None, None, None, :]
    )
    first = jnp.einsum("ai,ijkn->ajkn", deriv, cube, precision=HIGHEST)
    first = jnp.einsum("ai,ajkn->ijkn", deriv, geometry * first, precision=HIGHEST)
    second = jnp.einsum("bj,ijkn->ibkn", deriv, cube, precision=HIGHEST)
    second = jnp.einsum("bj,ibkn->ijkn", deriv, geometry * second, precision=HIGHEST)
    third = jnp.einsum("ck,ijkn->ijcn", deriv, cube, precision=HIGHEST)
    third = jnp.einsum("ck,ijcn->ijkn", deriv, geometry * third, precision=HIGHEST)
    return (first + second + third).reshape(NPTS**3, elems)


def extract_faces(local):
    elems = local.shape[1]
    cube = local.reshape(NPTS, NPTS, NPTS, elems)
    sides = jnp.stack(
        [
            cube[0],
            cube[NPTS - 1],
            cube[:, 0],
            cube[:, NPTS - 1],
            cube[:, :, 0],
            cube[:, :, NPTS - 1],
        ]
    )
    return sides.reshape(6, NPTS * NPTS, elems).transpose(1, 0, 2).reshape(NPTS * NPTS, 6 * elems)


def add_back(local, total):
    elems = local.shape[1]
    boxes = total.reshape(NPTS * NPTS, 6, elems).transpose(1, 0, 2).reshape(6, NPTS, NPTS, elems)
    cube = local.reshape(NPTS, NPTS, NPTS, elems)
    cube = cube.at[0].add(boxes[0]).at[NPTS - 1].add(boxes[1])
    cube = cube.at[:, 0].add(boxes[2]).at[:, NPTS - 1].add(boxes[3])
    cube = cube.at[:, :, 0].add(boxes[4]).at[:, :, NPTS - 1].add(boxes[5])
    return cube.reshape(NPTS**3, elems)


def pick_faces(faces, index_list):
    safe = jnp.maximum(index_list, 0)
    taken = jnp.take(faces, safe, axis=1)
    return taken * (index_list >= 0).astype(faces.dtype)[None, :]


def put_faces(total, index_list, values):
    safe = jnp.where(index_list >= 0, index_list, total.shape[1])
    return total.at[:, safe].add(values, mode="drop")


def restrict(face, part, halves):
    shape = face.shape
    grid = face.reshape(shape[:-2] + (NPTS, NPTS, shape[-1]))
    result = jnp.einsum(
        "ai,bj,...abn->...ijn", halves[part // 2], halves[part % 2], grid, precision=HIGHEST
    )
    return result.reshape(shape)


def prolong(face, part, halves):
    shape = face.shape
    grid = face.reshape(shape[:-2] + (NPTS, NPTS, shape[-1]))
    result = jnp.einsum(
        "ai,bj,...ijn->...abn", halves[part // 2], halves[part % 2], grid, precision=HIGHEST
    )
    return result.reshape(shape)


def near_step(values, offset):
    return from_behind(values, "dom", offset)


def far_step(values, offset):
    return from_behind(values, "dom", offset)


def body(
    nodal_values,
    kappa,
    levels,
    local_faces,
    sub_faces,
    near_faces,
    far_faces,
    child_faces,
    child_peer,
    coarse_faces,
):
    halves = jnp.asarray(node_tables(NPTS)[3], jnp.float32)
    local = stiffness(nodal_values, kappa, levels)
    faces = extract_faces(local)
    total = jnp.zeros_like(faces)
    total = put_faces(total, local_faces[0], pick_faces(faces, local_faces[1]))
    total = put_faces(total, local_faces[1], pick_faces(faces, local_faces[0]))
    rims = jnp.stack([pick_faces(faces, sub_faces[0]), pick_faces(faces, sub_faces[1])])
    padded = extended(rims, (("sub", 0),), 1)
    total = put_faces(total, sub_faces[0], padded[0])
    total = put_faces(total, sub_faces[1], padded[3])
    peers = lax.axis_size("dom")
    near_low = pick_faces(faces, near_faces[0])
    near_high = pick_faces(faces, near_faces[1])
    from_lower = near_step(near_high, 1)
    from_upper = near_step(near_low, -1)
    total = put_faces(total, near_faces[0], from_lower)
    total = put_faces(total, near_faces[1], from_upper)
    far_low = pick_faces(faces, far_faces[0])
    far_high = pick_faces(faces, far_faces[1])
    lower_parts = []
    upper_parts = []
    for step in range(SHIFTS):
        offset = step + 2
        lower_parts.append(far_step(far_high[:, step * FAR : (step + 1) * FAR], offset))
        upper_parts.append(far_step(far_low[:, step * FAR : (step + 1) * FAR], -offset))
    total = put_faces(total, far_faces[0], jnp.concatenate(lower_parts, axis=1))
    total = put_faces(total, far_faces[1], jnp.concatenate(upper_parts, axis=1))
    chosen = (child_peer[:, None] == lax.iota(jnp.int32, peers)[None, :]).astype(jnp.float32)
    children = jnp.stack([pick_faces(faces, child_faces[part]) for part in range(4)])
    coarse = pick_faces(faces, coarse_faces)
    projected = sum((restrict(children[part], part, halves) for part in range(4)))
    gathered = lax.all_to_all(
        jnp.dot(projected, chosen, precision=HIGHEST),
        "dom",
        split_axis=1,
        concat_axis=1,
        tiled=True,
    )
    summed = coarse + gathered
    returned = jnp.dot(
        lax.all_to_all(summed, "dom", split_axis=1, concat_axis=1, tiled=True),
        chosen.T,
        precision=HIGHEST,
    )
    for part in range(4):
        total = put_faces(
            total, child_faces[part], prolong(returned, part, halves) - children[part]
        )
    total = put_faces(total, coarse_faces, gathered)
    return add_back(local, total)


def solution(mesh):
    in_specs = (
        P(None, ("dom", "sub")),
        P(None, ("dom", "sub")),
        P(("dom", "sub")),
        P(None, ("dom", "sub")),
        P(None, ("dom", "sub")),
        P(None, ("dom", "sub")),
        P(None, ("dom", "sub")),
        P(None, ("dom", "sub")),
        P(("dom", "sub")),
        P(("dom", "sub")),
    )
    out_specs = P(None, ("dom", "sub"))
    return jax.shard_map(body, mesh=mesh, in_specs=in_specs, out_specs=out_specs, check_vma=False)
```

profile of v0, /device:TPU:26, one launch (start us, length us, event | category | flops | bytes accessed | tf_op | source)
XLA Modules:
  0.0 84.4 jit_solution(9114641115751658914)
XLA Ops:
  0.0 1.0 %copy-done = f32[512,256]{1,0:T(8,128)S(1)} copy-done((f32[512,256]{1,0:T(8,128)S(1)}, f32[512,256]{1,0:T(8,128)}, u32[]{:S(2)}) %copy-start) | copy-done | bytes 524312
  2.8 1.0 %convolution_multiply_fusion = f32[8,8,8,256]{3,0,2,1:T(8,128)S(1)} fusion(f32[8,8,1,1]{1,0,3,2:T(8,128)S(1)} %copy-done.2, f32[8,8,8,256]{3,2,1,0:T(8,128)S(1)} %bitcast.326, f32[8,8,8,256]{3,2,1,0:T(8,128)S(1)} %bitcast.343, f32[256]{0:T(256)S(1)} %convert_power_fusion, f32[8,8,8]{0,2,1:T(8,128)S(1)} %copy-done.3), kind=kOutput, calls=%fused_computation.28 | convolution fusion | flops 12976128 | bytes 1576192 | tf_op jit(solution)/shard_map/ai,ijkn->ajkn/dot_general | solution.py:96
  3.8 0.9 %bitcast_multiply_fusion.1 = (f32[8,8,8,256]{3,0,2,1:T(8,128)S(1)}, f32[8,8,8,256]{3,0,2,1:T(8,128)S(1)}) fusion(f32[8,8,8,256]{3,0,2,1:T(8,128)S(1)} %fusion.6, f32[8,8,8,256]{3,2,1,0:T(8,128)S(1)} %bitcast.344, f32[256]{0:T(256)S(1)} %convert_power_fusion, f32[8,8,8]{0,2,1:T(8,128)S(1)} %copy-done.3, f32[8,8,8,256]{3,0,2,1:T(8,128)S(1)} %fusion.99), kind=kLoop, calls=%fused_computation.38 | loop fusion | flops 524288 | bytes 2624512 | tf_op jit(solution)/shard_map/mul | solution.py:99
  5.5 0.9 %fusion.4 = f32[8,8,256,8]{2,3,1,0:T(8,128)S(1)} fusion(f32[8,8,1,1]{1,0,3,2:T(8,128)S(1)} %copy-done.2, f32[8,8,8,256]{3,0,2,1:T(8,128)S(1)} %get-tuple-element.105), kind=kOutput, calls=%fused_computation.41 | convolution fusion | flops 12582912 | bytes 1048832 | tf_op jit(solution)/shard_map/bj,ibkn->ijkn/dot_general | solution.py:99
  6.3 1.1 %fusion = f32[8,8,8,256]{3,0,2,1:T(8,128)S(1)} fusion(f32[8,8,1,1]{1,0,3,2:T(8,128)S(1)} %copy-done.2, f32[8,8,8,256]{3,0,2,1:T(8,128)S(1)} %convolution_multiply_fusion, f32[8,8,256,8]{2,3,1,0:T(8,128)S(1)} %fusion.2, f32[8,8,256,8]{2,3,1,0:T(8,128)S(1)} %fusion.4), kind=kOutput, calls=%fused_computation.27 | convolution fusion | flops 12845056 | bytes 2097408 | tf_op jit(solution)/shard_map/ai,ajkn->ijkn/dot_general | solution.py:97
  9.4 1.9 %collective-permute-start = (f32[1,64,32]{1,2,0:T(8,128)S(1)}, f32[1,64,32]{1,2,0:T(8,128)S(1)}, u32[]{:S(2)}, u32[]{:S(2)}) collective-permute-start(f32[1,64,32]{1,2,0:T(8,128)S(1)} %fusion.32), channel_id=1, source_target_pairs={{0,1},{1,2},{2,3},{4,5},{5,6},{6,7},{8,9},{9,10},{10,11},{12,13},{... | collective-permute-start | bytes 24584 | tf_op jit(solution)/shard_map/ppermute | solution.py:29
  12.0 3.6 %collective-permute-start.1 = (f32[1,64,32]{1,2,0:T(8,128)S(1)}, f32[1,64,32]{1,2,0:T(8,128)S(1)}, u32[]{:S(2)}, u32[]{:S(2)}) collective-permute-start(f32[1,64,32]{1,2,0:T(8,128)S(1)} %fusion.31), channel_id=1, source_target_pairs={{1,0},{2,1},{3,2},{5,4},{6,5},{7,6},{9,8},{10,9},{11,10},{13,12},{... | collective-permute-start | bytes 24584 | tf_op jit(solution)/shard_map/ppermute | solution.py:31
  16.3 3.4 %collective-permute-start.2 = (f32[64,32]{0,1:T(8,128)S(1)}, f32[64,32]{0,1:T(8,128)S(1)}, u32[]{:S(2)}, u32[]{:S(2)}) collective-permute-start(f32[64,32]{0,1:T(8,128)S(1)} %bitcast_multiply_fusion.7), channel_id=1, source_target_pairs={{0,4},{4,8},{8,12},{12,16},{16,20},{20,24},{24,28},{1,5},{5,9},{9,... | collective-permute-start | bytes 24584 | tf_op jit(solution)/shard_map/ppermute | solution.py:18
  20.4 3.3 %collective-permute-start.3 = (f32[64,32]{0,1:T(8,128)S(1)}, f32[64,32]{0,1:T(8,128)S(1)}, u32[]{:S(2)}, u32[]{:S(2)}) collective-permute-start(f32[64,32]{0,1:T(8,128)S(1)} %bitcast_multiply_fusion.6), channel_id=1, source_target_pairs={{4,0},{8,4},{12,8},{16,12},{20,16},{24,20},{28,24},{5,1},{9,5},{13... | collective-permute-start | bytes 24584 | tf_op jit(solution)/shard_map/ppermute | solution.py:18
  24.4 1.3 %collective-permute-start.6 = (f32[64,4]{0,1:T(4,128)S(1)}, f32[64,4]{0,1:T(4,128)S(1)}, u32[]{:S(2)}, u32[]{:S(2)}) collective-permute-start(f32[64,4]{0,1:T(4,128)S(1)} %get-tuple-element.123), channel_id=1, source_target_pairs={{0,16},{4,20},{8,24},{12,28},{1,17},{5,21},{9,25},{13,29},{2,18},{... | collective-permute-start | bytes 3080 | tf_op jit(solution)/shard_map/ppermute | solution.py:18
  32.8 6.8 %all-to-all-start = ((f32[64,8,1]{0,2,1:T(1,128)}), f32[64,8,1]{0,2,1:T(1,128)S(1)}, u32[]{:S(2)}, u32[]{:S(2)}) async-start(f32[64,8,1]{0,2,1:T(1,128)} %bitcast.92), calls=%async_computation | async-start | bytes 8192 | tf_op jit(solution)/shard_map/all_to_all | solution.py:211
  41.6 1.2 %all-to-all-done = f32[64,8,1]{0,2,1:T(1,128)S(1)} async-done(((f32[64,8,1]{0,2,1:T(1,128)}), f32[64,8,1]{0,2,1:T(1,128)S(1)}, u32[]{:S(2)}, u32[]{:S(2)}) %all-to-all-start) | async-done | bytes 2080 | tf_op jit(solution)/shard_map/all_to_all | solution.py:211
  43.4 6.5 %all-to-all-start.1 = ((f32[64,8,1]{0,2,1:T(1,128)}), f32[64,8,1]{0,2,1:T(1,128)S(1)}, u32[]{:S(2)}, u32[]{:S(2)}) async-start(f32[64,8,1]{0,2,1:T(1,128)} %bitcast.94), calls=%async_computation.1 | async-start | bytes 8192 | tf_op jit(solution)/shard_map/all_to_all | solution.py:220
  50.0 1.2 %scatter_custom_fusion = f32[64,1536]{0,1:T(8,128)S(1)} fusion(s32[64]{0:T(128)S(1)} %get-tuple-element.162, f32[]{:T(128)} %constant.229.clone.1, f32[]{:T(128)} %constant.233.clone.1, f32[64]{0:T(128)S(1)} %get-tuple-element.160, pred[64]{0:T(512)(128)(4,1)S(1)} %get-tuple-element.157, f32[64,1536]{0,1:T(8,128)S(1)} %bitcast.340, ...), kind=kCustom, calls=%fused_computation.48 | custom fusion | flops 12288 | bytes 1184776 | tf_op jit(solution)/shard_map/scatter-add | solution.py:139
  51.2 1.3 %scatter_custom_fusion.1 = f32[64,1536]{0,1:T(8,128)S(1)} fusion(f32[64,1536]{0,1:T(8,128)S(1)} %scatter_custom_fusion, s32[64]{0:T(128)S(1)} %get-tuple-element.161, f32[]{:T(128)} %constant.233.clone.1, f32[64]{0:T(128)S(1)} %get-tuple-element.159, pred[64]{0:T(512)(128)(4,1)S(1)} %get-tuple-element.101, f32[64,1536]{0,1:T(8,128)S(1)} %bitcast.341, ...), kind=kCustom, calls=%fused_computation.71 | custom fusion | flops 12288 | bytes 1184772 | tf_op jit(solution)/shard_map/scatter-add | solution.py:139
  54.6 1.3 %collective-permute-start.5 = (f32[64,4]{0,1:T(4,128)S(1)}, f32[64,4]{0,1:T(4,128)S(1)}, u32[]{:S(2)}, u32[]{:S(2)}) collective-permute-start(f32[64,4]{0,1:T(4,128)S(1)} %get-tuple-element.124), channel_id=1, source_target_pairs={{0,12},{4,16},{8,20},{12,24},{16,28},{1,13},{5,17},{9,21},{13,25},... | collective-permute-start | bytes 3080 | tf_op jit(solution)/shard_map/ppermute | solution.py:18
  55.9 1.3 %collective-permute-start.4 = (f32[64,4]{0,1:T(4,128)S(1)}, f32[64,4]{0,1:T(4,128)S(1)}, u32[]{:S(2)}, u32[]{:S(2)}) collective-permute-start(f32[64,4]{0,1:T(4,128)S(1)} %get-tuple-element.122), channel_id=1, source_target_pairs={{0,8},{4,12},{8,16},{12,20},{16,24},{20,28},{1,9},{5,13},{9,17},{1... | collective-permute-start | bytes 3080 | tf_op jit(solution)/shard_map/ppermute | solution.py:18
  57.2 7.0 %collective-permute-start.9 = (f32[64,4]{0,1:T(4,128)S(1)}, f32[64,4]{0,1:T(4,128)S(1)}, u32[]{:S(2)}, u32[]{:S(2)}) collective-permute-start(f32[64,4]{0,1:T(4,128)S(1)} %get-tuple-element.120), channel_id=1, source_target_pairs={{16,0},{20,4},{24,8},{28,12},{17,1},{21,5},{25,9},{29,13},{18,2},{... | collective-permute-start | bytes 3080 | tf_op jit(solution)/shard_map/ppermute | solution.py:18
  64.2 1.3 %collective-permute-start.8 = (f32[64,4]{0,1:T(4,128)S(1)}, f32[64,4]{0,1:T(4,128)S(1)}, u32[]{:S(2)}, u32[]{:S(2)}) collective-permute-start(f32[64,4]{0,1:T(4,128)S(1)} %get-tuple-element.121), channel_id=1, source_target_pairs={{12,0},{16,4},{20,8},{24,12},{28,16},{13,1},{17,5},{21,9},{25,13},... | collective-permute-start | bytes 3080 | tf_op jit(solution)/shard_map/ppermute | solution.py:18
  65.5 3.9 %collective-permute-start.7 = (f32[64,4]{0,1:T(4,128)S(1)}, f32[64,4]{0,1:T(4,128)S(1)}, u32[]{:S(2)}, u32[]{:S(2)}) collective-permute-start(f32[64,4]{0,1:T(4,128)S(1)} %get-tuple-element.119), channel_id=1, source_target_pairs={{8,0},{12,4},{16,8},{20,12},{24,16},{28,20},{9,1},{13,5},{17,9},{2... | collective-permute-start | bytes 3080 | tf_op jit(solution)/shard_map/ppermute | solution.py:18
  69.9 1.1 %scatter_custom_fusion.2 = f32[64,1536]{0,1:T(8,128)S(1)} fusion(f32[64,1536]{0,1:T(8,128)S(1)} %scatter_custom_fusion.1, s32[32]{0:T(128)S(1)} %get-tuple-element.156, f32[1,64,32]{1,2,0:T(8,128)S(1)} %collective-permute-done), kind=kCustom, calls=%fused_computation.80 | custom fusion | flops 2048 | bytes 409600 | tf_op jit(solution)/shard_map/scatter-add | solution.py:139
  71.0 1.0 %scatter_custom_fusion.3 = f32[64,1536]{0,1:T(8,128)S(1)} fusion(f32[64,1536]{0,1:T(8,128)S(1)} %scatter_custom_fusion.2, s32[32]{0:T(128)S(1)} %get-tuple-element.155, f32[1,64,32]{1,2,0:T(8,128)S(1)} %collective-permute-done.1), kind=kCustom, calls=%fused_computation.78 | custom fusion | flops 2048 | bytes 409600 | tf_op jit(solution)/shard_map/scatter-add | solution.py:139
  72.0 1.0 %scatter_custom_fusion.4 = f32[64,1536]{0,1:T(8,128)S(1)} fusion(f32[64,1536]{0,1:T(8,128)S(1)} %scatter_custom_fusion.3, s32[32]{0:T(128)S(1)} %get-tuple-element.150, f32[64,32]{0,1:T(8,128)S(1)} %collective-permute-done.2), kind=kCustom, calls=%fused_computation.85 | custom fusion | flops 2048 | bytes 409600 | tf_op jit(solution)/shard_map/scatter-add | solution.py:139
  73.1 1.0 %scatter_custom_fusion.5 = f32[64,1536]{0,1:T(8,128)S(1)} fusion(f32[64,1536]{0,1:T(8,128)S(1)} %scatter_custom_fusion.4, s32[32]{0:T(128)S(1)} %get-tuple-element.149, f32[64,32]{0,1:T(8,128)S(1)} %collective-permute-done.3), kind=kCustom, calls=%fused_computation.82 | custom fusion | flops 2048 | bytes 409600 | tf_op jit(solution)/shard_map/scatter-add | solution.py:139
  74.2 1.0 %scatter_custom_fusion.6 = f32[64,1536]{0,1:T(8,128)S(1)} fusion(f32[64,1536]{0,1:T(8,128)S(1)} %scatter_custom_fusion.5, s32[12]{0:T(128)S(1)} %get-tuple-element.144, f32[64,4]{0,1:T(4,128)S(1)} %collective-permute-done.6, f32[]{:T(128)} %constant.249, f32[64,4]{0,1:T(4,128)S(1)} %collective-permute-done.5, f32[64,4]{0,1:T(4,128)S(1)} %collective-permute-done.4), kind=kCustom, calls=%fused_computation.99 | custom fusion | flops 2304 | bytes 399364 | tf_op jit(solution)/shard_map/scatter-add | solution.py:139
  75.2 1.0 %scatter_custom_fusion.7 = f32[64,1536]{0,1:T(8,128)S(1)} fusion(f32[64,1536]{0,1:T(8,128)S(1)} %scatter_custom_fusion.6, s32[12]{0:T(128)S(1)} %get-tuple-element.143, f32[64,4]{0,1:T(4,128)S(1)} %collective-permute-done.9, f32[]{:T(128)} %constant.249, f32[64,4]{0,1:T(4,128)S(1)} %collective-permute-done.8, f32[64,4]{0,1:T(4,128)S(1)} %collective-permute-done.7), kind=kCustom, calls=%fused_computation.105 | custom fusion | flops 2304 | bytes 399364 | tf_op jit(solution)/shard_map/scatter-add | solution.py:139
  76.1 1.0 %scatter_custom_fusion.8 = f32[64,1536]{0,1:T(8,128)S(1)} fusion(f32[64,1536]{0,1:T(8,128)S(1)} %scatter_custom_fusion.7, s32[3]{0:T(128)S(1)} %get-tuple-element.128, f32[64,3]{0,1:T(4,128)S(1)} %reshape.714, f32[3,64]{1,0:T(4,128)S(1)} %gather_fusion.7, f32[3]{0:T(128)S(1)} %get-tuple-element.130, pred[3]{0:T(512)(128)(4,1)S(1)} %get-tuple-element.133), kind=kCustom, calls=%fused_computation.173 | custom fusion | flops 768 | bytes 398336 | tf_op jit(solution)/shard_map/scatter-add | solution.py:139
  77.1 1.0 %scatter_custom_fusion.9 = f32[64,1536]{0,1:T(8,128)S(1)} fusion(f32[64,1536]{0,1:T(8,128)S(1)} %scatter_custom_fusion.8, s32[3]{0:T(128)S(1)} %get-tuple-element.126, f32[64,3]{0,1:T(4,128)S(1)} %reshape.715, f32[3,64]{1,0:T(4,128)S(1)} %gather_fusion.8, f32[3]{0:T(128)S(1)} %get-tuple-element.131, pred[3]{0:T(512)(128)(4,1)S(1)} %get-tuple-element.135), kind=kCustom, calls=%fused_computation.171 | custom fusion | flops 768 | bytes 398336 | tf_op jit(solution)/shard_map/scatter-add | solution.py:139
  78.1 1.0 %scatter_custom_fusion.10 = f32[64,1536]{0,1:T(8,128)S(1)} fusion(f32[64,1536]{0,1:T(8,128)S(1)} %scatter_custom_fusion.9, s32[3]{0:T(128)S(1)} %get-tuple-element.127, f32[64,3]{0,1:T(4,128)S(1)} %reshape.716, f32[3,64]{1,0:T(4,128)S(1)} %gather_fusion.9, f32[3]{0:T(128)S(1)} %get-tuple-element.132, pred[3]{0:T(512)(128)(4,1)S(1)} %get-tuple-element.137), kind=kCustom, calls=%fused_computation.169 | custom fusion | flops 768 | bytes 398336 | tf_op jit(solution)/shard_map/scatter-add | solution.py:139
  79.1 1.0 %scatter_custom_fusion.11 = f32[64,1536]{0,1:T(8,128)S(1)} fusion(f32[64,1536]{0,1:T(8,128)S(1)} %scatter_custom_fusion.10, s32[3]{0:T(128)S(1)} %get-tuple-element.125, f32[64,3]{0,1:T(4,128)S(1)} %reshape.717, f32[3,64]{1,0:T(4,128)S(1)} %gather_fusion.10, f32[3]{0:T(128)S(1)} %get-tuple-element.129, pred[3]{0:T(512)(128)(4,1)S(1)} %get-tuple-element.81), kind=kCustom, calls=%fused_computation.167 | custom fusion | flops 768 | bytes 398336 | tf_op jit(solution)/shard_map/scatter-add | solution.py:139
  80.1 0.9 %scatter_fusion = f32[64,1536]{0,1:T(8,128)S(1)} fusion(f32[64,1536]{0,1:T(8,128)S(1)} %scatter_custom_fusion.11, s32[8]{0:T(128)S(1)} %get-tuple-element.163, f32[8,64]{1,0:T(8,128)S(1)} %bitcast.348), kind=kCustom, calls=%fused_computation.25 | custom fusion | flops 512 | bytes 6176 | tf_op jit(solution)/shard_map/scatter-add | solution.py:139
  83.5 1.0 %copy.135 = f32[8,8,8,256]{3,2,1,0:T(8,128)} copy(f32[8,8,8,256]{3,0,2,1:T(8,128)S(1)} %fusion.12) | data formatting | bytes 1048576 | tf_op jit(solution)/shard_map/scatter-add | solution.py:127
  (140 shorter events, 21.3 us)
Async XLA Ops:
  0.0 1.0 %copy-start = (f32[512,256]{1,0:T(8,128)S(1)}, f32[512,256]{1,0:T(8,128)}, u32[]{:S(2)}) copy-start(f32[512,256]{1,0:T(8,128)} %param.33) | copy-start | bytes 1572868
  0.0 1.0 %copy-start.2 = (f32[8,8,1,1]{1,0,3,2:T(8,128)S(1)}, f32[8,8,1,1]{1,0,3,2:T(8,128)}, u32[]{:S(2)}) copy-start(f32[8,8,1,1]{1,0,3,2:T(8,128)} %constant.246) | copy-start | bytes 772
  1.7 0.7 copy-start.11
  1.7 1.0 %copy-start.1 = (f32[512,256]{1,0:T(8,128)S(1)}, f32[512,256]{1,0:T(8,128)}, u32[]{:S(2)}) copy-start(f32[512,256]{1,0:T(8,128)} %param.34) | copy-start | bytes 1572868
  1.7 1.0 %copy-start.3 = (f32[8,8,8]{0,2,1:T(8,128)S(1)}, f32[8,8,8]{0,2,1:T(8,128)}, u32[]{:S(2)}) copy-start(f32[8,8,8]{0,2,1:T(8,128)} %constant.237.clone) | copy-start | bytes 6148
  7.6 0.7 copy-start.9
  7.6 0.7 copy-start.10
  9.4 46.5 %collective-permute-start = (f32[1,64,32]{1,2,0:T(8,128)S(1)}, f32[1,64,32]{1,2,0:T(8,128)S(1)}, u32[]{:S(2)}, u32[]{:S(2)}) collective-permute-start(f32[1,64,32]{1,2,0:T(8,128)S(1)} %fusion.32), channel_id=1, source_target_pairs={{0,1},{1,2},{2,3},{4,5},{5,6},{6,7},{8,9},{9,10},{10,11},{12,13},{... | collective-permute-start | bytes 24584 | tf_op jit(solution)/shard_map/ppermute | solution.py:29
  12.0 45.2 %collective-permute-start.1 = (f32[1,64,32]{1,2,0:T(8,128)S(1)}, f32[1,64,32]{1,2,0:T(8,128)S(1)}, u32[]{:S(2)}, u32[]{:S(2)}) collective-permute-start(f32[1,64,32]{1,2,0:T(8,128)S(1)} %fusion.31), channel_id=1, source_target_pairs={{1,0},{2,1},{3,2},{5,4},{6,5},{7,6},{9,8},{10,9},{11,10},{13,12},{... | collective-permute-start | bytes 24584 | tf_op jit(solution)/shard_map/ppermute | solution.py:31
  16.3 47.9 %collective-permute-start.2 = (f32[64,32]{0,1:T(8,128)S(1)}, f32[64,32]{0,1:T(8,128)S(1)}, u32[]{:S(2)}, u32[]{:S(2)}) collective-permute-start(f32[64,32]{0,1:T(8,128)S(1)} %bitcast_multiply_fusion.7), channel_id=1, source_target_pairs={{0,4},{4,8},{8,12},{12,16},{16,20},{20,24},{24,28},{1,5},{5,9},{9,... | collective-permute-start | bytes 24584 | tf_op jit(solution)/shard_map/ppermute | solution.py:18
  20.3 3.4 %copy-start.8 = (s32[2,12]{1,0:T(2,128)S(1)}, s32[2,12]{1,0:T(2,128)}, u32[]{:S(2)}) copy-start(s32[2,12]{1,0:T(2,128)} %param.39) | copy-start | bytes 292
  20.4 45.1 %collective-permute-start.3 = (f32[64,32]{0,1:T(8,128)S(1)}, f32[64,32]{0,1:T(8,128)S(1)}, u32[]{:S(2)}, u32[]{:S(2)}) collective-permute-start(f32[64,32]{0,1:T(8,128)S(1)} %bitcast_multiply_fusion.6), channel_id=1, source_target_pairs={{4,0},{8,4},{12,8},{16,12},{20,16},{24,20},{28,24},{5,1},{9,5},{13... | collective-permute-start | bytes 24584 | tf_op jit(solution)/shard_map/ppermute | solution.py:18
  23.8 1.9 %copy-start.6 = (s32[4,3]{1,0:T(4,128)S(1)}, s32[4,3]{1,0:T(4,128)}, u32[]{:S(2)}) copy-start(s32[4,3]{1,0:T(4,128)} %param.40) | copy-start | bytes 148
  24.4 30.2 %collective-permute-start.6 = (f32[64,4]{0,1:T(4,128)S(1)}, f32[64,4]{0,1:T(4,128)S(1)}, u32[]{:S(2)}, u32[]{:S(2)}) collective-permute-start(f32[64,4]{0,1:T(4,128)S(1)} %get-tuple-element.123), channel_id=1, source_target_pairs={{0,16},{4,20},{8,24},{12,28},{1,17},{5,21},{9,25},{13,29},{2,18},{... | collective-permute-start | bytes 3080 | tf_op jit(solution)/shard_map/ppermute | solution.py:18
  26.4 0.7 copy-start.5
  29.8 0.7 copy-start.4
  31.3 0.7 copy-start.13
  32.8 6.8 %copy-start.7 = (s32[2,64]{1,0:T(2,128)S(1)}, s32[2,64]{1,0:T(2,128)}, u32[]{:S(2)}) copy-start(s32[2,64]{1,0:T(2,128)} %param.36) | copy-start | bytes 1540
  32.8 9.9 %all-to-all-start = ((f32[64,8,1]{0,2,1:T(1,128)}), f32[64,8,1]{0,2,1:T(1,128)S(1)}, u32[]{:S(2)}, u32[]{:S(2)}) async-start(f32[64,8,1]{0,2,1:T(1,128)} %bitcast.92), calls=%async_computation | async-start | bytes 8192 | tf_op jit(solution)/shard_map/all_to_all | solution.py:211
  39.7 0.7 copy-start.12
  43.4 9.7 %all-to-all-start.1 = ((f32[64,8,1]{0,2,1:T(1,128)}), f32[64,8,1]{0,2,1:T(1,128)S(1)}, u32[]{:S(2)}, u32[]{:S(2)}) async-start(f32[64,8,1]{0,2,1:T(1,128)} %bitcast.94), calls=%async_computation.1 | async-start | bytes 8192 | tf_op jit(solution)/shard_map/all_to_all | solution.py:220
  54.6 19.6 %collective-permute-start.5 = (f32[64,4]{0,1:T(4,128)S(1)}, f32[64,4]{0,1:T(4,128)S(1)}, u32[]{:S(2)}, u32[]{:S(2)}) collective-permute-start(f32[64,4]{0,1:T(4,128)S(1)} %get-tuple-element.124), channel_id=1, source_target_pairs={{0,12},{4,16},{8,20},{12,24},{16,28},{1,13},{5,17},{9,21},{13,25},... | collective-permute-start | bytes 3080 | tf_op jit(solution)/shard_map/ppermute | solution.py:18
  55.9 18.2 %collective-permute-start.4 = (f32[64,4]{0,1:T(4,128)S(1)}, f32[64,4]{0,1:T(4,128)S(1)}, u32[]{:S(2)}, u32[]{:S(2)}) collective-permute-start(f32[64,4]{0,1:T(4,128)S(1)} %get-tuple-element.122), channel_id=1, source_target_pairs={{0,8},{4,12},{8,16},{12,20},{16,24},{20,28},{1,9},{5,13},{9,17},{1... | collective-permute-start | bytes 3080 | tf_op jit(solution)/shard_map/ppermute | solution.py:18
  57.2 17.9 %collective-permute-start.9 = (f32[64,4]{0,1:T(4,128)S(1)}, f32[64,4]{0,1:T(4,128)S(1)}, u32[]{:S(2)}, u32[]{:S(2)}) collective-permute-start(f32[64,4]{0,1:T(4,128)S(1)} %get-tuple-element.120), channel_id=1, source_target_pairs={{16,0},{20,4},{24,8},{28,12},{17,1},{21,5},{25,9},{29,13},{18,2},{... | collective-permute-start | bytes 3080 | tf_op jit(solution)/shard_map/ppermute | solution.py:18
  64.2 10.9 %collective-permute-start.8 = (f32[64,4]{0,1:T(4,128)S(1)}, f32[64,4]{0,1:T(4,128)S(1)}, u32[]{:S(2)}, u32[]{:S(2)}) collective-permute-start(f32[64,4]{0,1:T(4,128)S(1)} %get-tuple-element.121), channel_id=1, source_target_pairs={{12,0},{16,4},{20,8},{24,12},{28,16},{13,1},{17,5},{21,9},{25,13},... | collective-permute-start | bytes 3080 | tf_op jit(solution)/shard_map/ppermute | solution.py:18
  65.5 9.6 %collective-permute-start.7 = (f32[64,4]{0,1:T(4,128)S(1)}, f32[64,4]{0,1:T(4,128)S(1)}, u32[]{:S(2)}, u32[]{:S(2)}) collective-permute-start(f32[64,4]{0,1:T(4,128)S(1)} %get-tuple-element.119), channel_id=1, source_target_pairs={{8,0},{12,4},{16,8},{20,12},{24,16},{28,20},{9,1},{13,5},{17,9},{2... | collective-permute-start | bytes 3080 | tf_op jit(solution)/shard_map/ppermute | solution.py:18
where the time goes:
time: 85 us; the launch traced here: 84.4 us
  starting transfers between devices  41.7 us (49%)
  other arithmetic  16.3 us (19%)
  local copies, waits for them, and re-layouts  15.2 us (18%)
  matrix products  8.67 us (10%)
  waiting for transfers between devices  1.75 us (2%)
    ppermute x8, starting transfers between devices, from_behind(): return lax.ppermute(block, axis, route)  22.8 us
    scatter-add x13, other arithmetic, put_faces(): return total.at[:, safe].add(values, mode='drop')  13.6 us
    all_to_all x1, starting transfers between devices, body(): lax.all_to_all(jnp.dot(projected, chosen, precision=HIGHEST), 'dom', spli...  6.8 us
    all_to_all x1, starting transfers between devices, body(): lax.all_to_all(summed, 'dom', split_axis=1, concat_axis=1, tiled=True)  6.53 us
    gather x11, local copies, waits for them, and re-layouts, pick_faces(): taken = jnp.take(faces, safe, axis=1)  6.22 us
    unnamed x33, local copies, waits for them, and re-layouts  4.7 us
    ppermute x1, starting transfers between devices, extended(): lax.ppermute(head, axis, [((i + 1) % count, i) for i in range(ends)])  3.64 us
    ppermute x1, starting transfers between devices, extended(): lax.ppermute(tail, axis, [(i, (i + 1) % count) for i in range(ends)])  1.91 us
  transfers between devices with their start and end apart: 12, of which 2 were waited for; matrix products, arithmetic and copies ran while one was open for 23% of the time, Pallas kernels for 0%

commit v1 on v0

v1 whole, which is shorter than its diff:
```python
import functools

import jax
import jax.numpy as jnp
import numpy as np
from jax import lax
from jax.experimental import pallas as pl
from jax.experimental.pallas import tpu as pltpu
from jax.sharding import PartitionSpec as P

NPTS = 8
FAR = 4
MESH = pl.DeviceIdType.MESH
F32, BF16, I32 = jnp.float32, jnp.bfloat16, jnp.int32


def legendre_table(points, degree):
    table = [np.ones(points.shape), points.copy()]
    for order in range(2, degree + 1):
        table.append(
            ((2 * order - 1) * points * table[order - 1] - (order - 1) * table[order - 2]) / order
        )
    return table


def lobatto_points(degree):
    points = np.cos(np.pi * np.arange(degree + 1) / degree)
    for sweep in range(100):
        table = legendre_table(points, degree)
        points = points - (points * table[degree] - table[degree - 1]) / (
            (degree + 1) * table[degree]
        )
    points = np.sort(points)
    return (points, legendre_table(points, degree)[degree])


def node_tables(count):
    degree = count - 1
    points, legendre = lobatto_points(degree)
    weights = 2.0 / (degree * (degree + 1) * legendre**2)
    spread = points[:, None] - points[None, :] + np.eye(count)
    derivative = legendre[:, None] / (legendre[None, :] * spread) * (1.0 - np.eye(count))
    derivative[0, 0] = -degree * (degree + 1) / 4.0
    derivative[degree, degree] = degree * (degree + 1) / 4.0
    halves = []
    for side in range(2):
        target = (points + 2.0 * side - 1.0) / 2.0
        matrix = np.ones((count, count))
        for column in range(count):
            for other in range(count):
                if other != column:
                    matrix[:, column] = (
                        matrix[:, column]
                        * (target - points[other])
                        / (points[column] - points[other])
                    )
        halves.append(matrix)
    return (points, weights, derivative, np.stack(halves))


POINTS, WEIGHTS, DERIV, HALVES = node_tables(NPTS)


def up(count, unit=8):
    return -(-count // unit) * unit


def halves_of(values):
    high = values.astype(BF16)
    return high, (values - high.astype(F32)).astype(BF16)


def numpy_halves(matrix):
    matrix = np.asarray(matrix, np.float32)
    high = matrix.astype(jnp.bfloat16)
    low = (matrix - high.astype(np.float32)).astype(jnp.bfloat16)
    return high, low


def dot(a, b, dims=((1,), (0,))):
    return lax.dot_general(a, b, (dims, ((), ())), preferred_element_type=F32)


def select(hot, values):
    high, low = halves_of(values)
    return dot(hot, high) + dot(hot, low)


def take_rows(hot, face):
    high, low = halves_of(face)
    dims = ((1,), (1,))
    return dot(hot, high, dims) + dot(hot, low, dims)


def spread_rows(rows, hot):
    high, low = halves_of(rows.T)
    return dot(high, hot) + dot(low, hot)


def product(a, matrix):
    high, low = halves_of(a)
    mhigh, mlow = halves_of(matrix)
    return dot(high, mhigh) + dot(low, mhigh) + dot(high, mlow)


def column(row, padded):
    count = row.shape[1]
    r = lax.broadcasted_iota(I32, (padded, count), 0)
    c = lax.broadcasted_iota(I32, (padded, count), 1)
    spread = jnp.where(r == c, jnp.broadcast_to(row.astype(F32), (padded, count)), 0.0)
    col = jnp.sum(spread, axis=1, keepdims=True)
    inside = lax.broadcasted_iota(I32, (padded, 1), 0) < count
    return jnp.where(inside, col, -1.0)


def hot_rows(columns, base, elems):
    col = columns[0] if len(columns) == 1 else jnp.concatenate(columns, axis=0)
    lane = lax.broadcasted_iota(I32, (col.shape[0], elems), 1).astype(F32)
    return jnp.where(lane == col - float(base), 1.0, 0.0).astype(BF16)


def line(values, matrix):
    half = NPTS // 2
    even = [values[i] + values[NPTS - 1 - i] for i in range(half)]
    odd = [values[i] - values[NPTS - 1 - i] for i in range(half)]
    out = [None] * NPTS
    for a in range(half):
        p = q = None
        for i in range(half):
            s = float((matrix[a, i] + matrix[a, NPTS - 1 - i]) / 2)
            t = float((matrix[a, i] - matrix[a, NPTS - 1 - i]) / 2)
            p = even[i] * s if p is None else p + even[i] * s
            q = odd[i] * t if q is None else q + odd[i] * t
        out[a] = q + p
        out[NPTS - 1 - a] = q - p
    return out


def stencil(matrix):
    big = np.kron(np.eye(16), matrix)
    high, low = numpy_halves(big)
    return np.concatenate([high, high], axis=1), low


def kernel(
    sizes,
    u_hbm,
    kappa_hbm,
    level_hbm,
    local_hbm,
    sub_hbm,
    near_hbm,
    far_hbm,
    child_hbm,
    coarse_hbm,
    deriv_hbm,
    mortar_hbm,
    peer_ref,
    out_hbm,
    level_ref,
    local_ref,
    sub_ref,
    near_ref,
    far_ref,
    child_ref,
    coarse_ref,
    deriv_ref,
    mortar_ref,
    w_ref,
    u_ref,
    k_ref,
    g_ref,
    side_out,
    side_in,
    msg_out,
    msg_in,
    small_sem,
    load_sem,
    side_send,
    side_recv,
    msg_send,
    msg_recv,
):
    n_dom, n_sub = sizes
    parts = u_ref.shape[0]
    elems = parts * 128
    me, sub = lax.axis_index("dom"), lax.axis_index("sub")

    small = [
        pltpu.make_async_copy(source, target, small_sem.at[slot])
        for slot, (source, target) in enumerate(
            [
                (local_hbm, local_ref),
                (sub_hbm, sub_ref),
                (near_hbm, near_ref),
                (far_hbm, far_ref),
                (child_hbm, child_ref),
                (coarse_hbm, coarse_ref),
                (level_hbm, level_ref),
                (deriv_hbm, deriv_ref),
                (mortar_hbm, mortar_ref),
            ]
        )
    ]
    for copy in small[:7]:
        copy.start()

    def load(n, source, target, slot):
        block = source.at[:, pl.ds(n * 128, 128)]
        return pltpu.make_async_copy(block, target.at[n], load_sem.at[slot, n])

    for n in range(parts):
        load(n, u_hbm, u_ref, 0).start()
        load(n, kappa_hbm, k_ref, 1).start()
    for copy in small[7:]:
        copy.start()

    barrier = pltpu.get_barrier_semaphore()

    def greet(step, carry):
        other = lax.rem(me + step, n_dom)
        pl.semaphore_signal(barrier, inc=1, device_id=(other, sub), device_id_type=MESH)
        return carry

    lax.fori_loop(1, n_dom, greet, 0, unroll=n_dom <= 8)

    @pl.when(sub > 0)
    def _():
        pl.semaphore_signal(barrier, inc=1, device_id=(me, sub - 1), device_id_type=MESH)

    @pl.when(sub < n_sub - 1)
    def _():
        pl.semaphore_signal(barrier, inc=1, device_id=(me, sub + 1), device_id_type=MESH)

    def clear(missing, slot):
        @pl.when(missing)
        def _():
            side_in[slot] = jnp.zeros(side_in.shape[1:], F32)

    clear(sub == 0, 0)
    clear(sub == n_sub - 1, 1)
    clear(me == 0, 2)
    clear(me == n_dom - 1, 3)
    msg_in[me] = jnp.zeros(msg_in.shape[1:], F32)

    for copy in small[:7]:
        copy.wait()

    pairs, rim, near = local_ref.shape[1], sub_ref.shape[1], near_ref.shape[1]
    far, groups = far_ref.shape[1], child_ref.shape[1]
    farp, groupp, coarsep = up(far), up(groups), up(n_dom)
    hot0l = hot_rows([column(local_ref[1:2], up(pairs))], 0, elems)
    hot1l = hot_rows([column(local_ref[0:1], up(pairs))], elems, elems)
    hot0s = hot_rows([column(sub_ref[0:1], up(rim))], 0, elems)
    hot1s = hot_rows([column(sub_ref[1:2], up(rim))], elems, elems)
    hot2 = hot_rows([column(near_ref[0:1], up(near))], 2 * elems, elems)
    hot3 = hot_rows([column(near_ref[1:2], up(near))], 3 * elems, elems)
    children = [column(child_ref[m : m + 1], groupp) for m in range(4)]
    hot4 = hot_rows([column(far_ref[0:1], farp)] + children, 4 * elems, elems)
    hot5 = hot_rows(
        [column(far_ref[1:2], farp), column(coarse_ref[...], coarsep)], 5 * elems, elems
    )

    sources = 2 * farp + groupp + coarsep
    rows = 8 * n_dom

    def keys(shape, dim, group_slot, coarse_slot):
        c = lax.broadcasted_iota(I32, shape, dim)
        h = c - farp
        f = jnp.where(c < farp, c, h)
        s, j = lax.shift_right_logical(f, 2), lax.bitwise_and(f, FAR - 1)
        gap = jnp.where(c < farp, -2 - s, s + 2)
        key = jnp.where(f < far, (me + gap) * 8 + j, -1)
        key = jnp.where(c >= 2 * farp, -1, key)
        first = 2 * farp + groupp
        key = jnp.where(c >= first, (c - first) * 8 + coarse_slot, key)
        for slot in range(groups):
            key = jnp.where(c == 2 * farp + slot, peer_ref[slot] * 8 + group_slot, key)
        return key

    def hot(mask):
        return jnp.where(mask, 1.0, 0.0).astype(BF16)

    route = hot(
        lax.broadcasted_iota(I32, (rows, sources), 0) == keys((1, sources), 1, 4, 5)
    )
    unroute = hot(
        lax.broadcasted_iota(I32, (sources, rows), 1) == keys((sources, 1), 0, 5, 4)
    )

    scale = jnp.exp2(-level_ref[...].astype(F32))
    sub8 = lax.broadcasted_iota(I32, (8, elems), 0)
    weight = jnp.zeros((8, elems), F32)
    for k in range(NPTS):
        weight = jnp.where(sub8 == k, float(WEIGHTS[k]), weight)
    weight = weight * scale

    def slab(i, j):
        return pl.ds((i * NPTS + j) * NPTS, NPTS)

    def across(ref, own):
        return jnp.concatenate([ref[n, own, :] for n in range(parts)], axis=1)

    def add_across(own, values):
        for n in range(parts):
            w_ref[n, own, :] += values[:, n * 128 : (n + 1) * 128]

    for n in range(parts):
        load(n, u_hbm, u_ref, 0).wait()
        load(n, kappa_hbm, k_ref, 1).wait()
        here = weight[:, n * 128 : (n + 1) * 128]
        for j in range(NPTS):
            flux = line([u_ref[n, slab(i, j), :] for i in range(NPTS)], DERIV)
            for i in range(NPTS):
                g = k_ref[n, slab(i, j), :] * (here * float(WEIGHTS[i] * WEIGHTS[j]))
                g_ref[n, slab(i, j), :] = g
                flux[i] = flux[i] * g
            flux = line(flux, DERIV.T)
            for i in range(NPTS):
                w_ref[n, slab(i, j), :] = flux[i]
        for i in range(NPTS):
            flux = line([u_ref[n, slab(i, j), :] for j in range(NPTS)], DERIV)
            flux = [flux[j] * g_ref[n, slab(i, j), :] for j in range(NPTS)]
            flux = line(flux, DERIV.T)
            for j in range(NPTS):
                w_ref[n, slab(i, j), :] += flux[j]
    for copy in small[7:]:
        copy.wait()
    block = 128
    for part in range(NPTS**3 // block):
        own = pl.ds(part * block, block)
        high, low = halves_of(across(u_ref, own))
        flux = dot(deriv_ref[0:block, 0 : 2 * block], jnp.concatenate([high, low], axis=0))
        flux += dot(deriv_ref[0:block, 2 * block : 3 * block], high)
        high, low = halves_of(flux * across(g_ref, own))
        turn = dot(deriv_ref[block : 2 * block, 0 : 2 * block], jnp.concatenate([high, low], axis=0))
        turn += dot(deriv_ref[block : 2 * block, 2 * block : 3 * block], high)
        add_across(own, turn)

    square = NPTS * NPTS
    last = NPTS - 1
    low_i, high_i = pl.ds(0, square), pl.ds(last * square, square)
    low_k, high_k = pl.ds(0, square, NPTS), pl.ds(last, square, NPTS)
    face0 = across(w_ref, low_i)
    face1 = across(w_ref, high_i)
    face2 = jnp.concatenate([across(w_ref, slab(i, 0)) for i in range(NPTS)], axis=0)
    face3 = jnp.concatenate([across(w_ref, slab(i, last)) for i in range(NPTS)], axis=0)
    face4 = across(w_ref, low_k)
    face5 = across(w_ref, high_k)

    taken4 = take_rows(hot4, face4)
    taken5 = take_rows(hot5, face5)
    family = [taken4[farp + m * groupp : farp + (m + 1) * groupp] for m in range(4)]
    down = [mortar_ref[m * square : (m + 1) * square, 0:square] for m in range(4)]
    lift = [mortar_ref[m * square : (m + 1) * square, square:] for m in range(4)]
    projected = sum(product(family[m], down[m]) for m in range(4))
    source = jnp.concatenate(
        [taken4[0:farp], taken5[0:farp], projected, taken5[farp:]], axis=0
    )
    message = select(route, source)
    for p in range(n_dom):
        msg_out[p, :, 0:square] = message[8 * p : 8 * p + 8]
    side_out[0, 0:rim, 0:square] = take_rows(hot0s, face0)[0:rim]
    side_out[1, 0:rim, 0:square] = take_rows(hot1s, face1)[0:rim]
    side_out[2, 0:near, 0:square] = take_rows(hot2, face2)[0:near]
    side_out[3, 0:near, 0:square] = take_rows(hot3, face3)[0:near]

    pl.semaphore_wait(
        barrier, n_dom - 1 + (sub > 0).astype(I32) + (sub < n_sub - 1).astype(I32)
    )

    def post(step):
        other = lax.rem(me + step, n_dom)
        return pltpu.make_async_remote_copy(
            src_ref=msg_out.at[other],
            dst_ref=msg_in.at[me],
            send_sem=msg_send.at[other],
            recv_sem=msg_recv.at[me],
            device_id=(other, sub),
            device_id_type=MESH,
        )

    def arrival(step):
        other = lax.rem(me + step, n_dom)
        return pltpu.make_async_remote_copy(
            src_ref=msg_out.at[other],
            dst_ref=msg_in.at[other],
            send_sem=msg_send.at[other],
            recv_sem=msg_recv.at[other],
            device_id=(other, sub),
            device_id_type=MESH,
        )

    sides = [
        (sub > 0, 0, 1, (me, sub - 1)),
        (sub < n_sub - 1, 1, 0, (me, sub + 1)),
        (me > 0, 2, 3, (me - 1, sub)),
        (me < n_dom - 1, 3, 2, (me + 1, sub)),
    ]

    def side_copy(mine, theirs, device):
        return pltpu.make_async_remote_copy(
            src_ref=side_out.at[mine],
            dst_ref=side_in.at[theirs],
            send_sem=side_send.at[mine],
            recv_sem=side_recv.at[theirs],
            device_id=device,
            device_id_type=MESH,
        )

    def start_all(step, carry):
        post(step).start()
        return carry

    lax.fori_loop(1, n_dom, start_all, 0, unroll=n_dom <= 8)
    for there, mine, theirs, device in sides:
        @pl.when(there)
        def _():
            side_copy(mine, theirs, device).start()

    add_across(low_i, spread_rows(take_rows(hot1l, face1), hot0l))
    add_across(high_i, spread_rows(take_rows(hot0l, face0), hot1l))

    for there, mine, theirs, device in sides:
        @pl.when(there)
        def _():
            side_copy(mine, mine, device).wait()

    add_across(low_i, spread_rows(side_in[0, 0:rim, 0:square], hot0s))
    add_across(high_i, spread_rows(side_in[1, 0:rim, 0:square], hot1s))
    add2 = spread_rows(side_in[2, 0:near, 0:square], hot2)
    add3 = spread_rows(side_in[3, 0:near, 0:square], hot3)
    for i in range(NPTS):
        add_across(slab(i, 0), add2[i * NPTS : (i + 1) * NPTS])
        add_across(slab(i, last), add3[i * NPTS : (i + 1) * NPTS])

    def wait_all(step, carry):
        arrival(step).wait()
        return carry

    lax.fori_loop(1, n_dom, wait_all, 0, unroll=n_dom <= 8)
    received = jnp.concatenate([msg_in[p, :, 0:square] for p in range(n_dom)], axis=0)
    back = select(unroute, received)
    summed = back[2 * farp : 2 * farp + groupp] + projected
    add4 = [back[0:farp]] + [product(summed, lift[m]) - family[m] for m in range(4)]
    add5 = [back[farp : 2 * farp], back[2 * farp + groupp :]]
    add_across(low_k, spread_rows(jnp.concatenate(add4, axis=0), hot4))
    add_across(high_k, spread_rows(jnp.concatenate(add5, axis=0), hot5))

    def store(n):
        block = out_hbm.at[:, pl.ds(n * 128, 128)]
        return pltpu.make_async_copy(w_ref.at[n], block, load_sem.at[0, n])

    for n in range(parts):
        store(n).start()
    for n in range(parts):
        store(n).wait()


def body(
    sizes,
    nodal_values,
    kappa,
    levels,
    local_faces,
    sub_faces,
    near_faces,
    far_faces,
    child_faces,
    child_peer,
    coarse_faces,
):
    n_dom, n_sub = sizes
    elems = nodal_values.shape[1]
    double, single = stencil(DERIV)
    double_t, single_t = stencil(DERIV.T)
    deriv = np.concatenate(
        [np.concatenate([double, single], 1), np.concatenate([double_t, single_t], 1)], 0
    )
    krons = [np.kron(HALVES[m // 2], HALVES[m % 2]) for m in range(4)]
    mortar = np.concatenate([np.concatenate([m, m.T], axis=1) for m in krons], axis=0)
    held = (elems // 128, NPTS**3, 128)
    side_rows = up(max(sub_faces.shape[1], near_faces.shape[1]))
    small = [
        levels.reshape(1, elems),
        local_faces,
        sub_faces,
        near_faces,
        far_faces,
        child_faces,
        coarse_faces.reshape(1, n_dom),
        jnp.asarray(deriv, BF16),
        jnp.asarray(mortar, F32),
    ]
    smem = pl.BlockSpec(memory_space=pltpu.SMEM)
    hbm = pl.BlockSpec(memory_space=pl.ANY)
    return pl.pallas_call(
        functools.partial(kernel, sizes),
        out_shape=jax.ShapeDtypeStruct(nodal_values.shape, F32),
        in_specs=[hbm] * 11 + [smem],
        out_specs=hbm,
        scratch_shapes=[pltpu.VMEM(item.shape, item.dtype) for item in small]
        + [
            pltpu.VMEM(held, F32),
            pltpu.VMEM(held, F32),
            pltpu.VMEM(held, F32),
            pltpu.VMEM(held, F32),
            pltpu.VMEM((4, side_rows, 128), F32),
            pltpu.VMEM((4, side_rows, 128), F32),
            pltpu.VMEM((n_dom, 8, 128), F32),
            pltpu.VMEM((n_dom, 8, 128), F32),
            pltpu.SemaphoreType.DMA((len(small),)),
            pltpu.SemaphoreType.DMA((2, held[0])),
            pltpu.SemaphoreType.DMA((4,)),
            pltpu.SemaphoreType.DMA((4,)),
            pltpu.SemaphoreType.DMA((n_dom,)),
            pltpu.SemaphoreType.DMA((n_dom,)),
        ],
        compiler_params=pltpu.CompilerParams(
            collective_id=0, has_side_effects=True, vmem_limit_bytes=60 * 1024 * 1024
        ),
    )(
        nodal_values,
        kappa,
        *small,
        child_peer,
    )


def solution(mesh):
    sizes = (mesh.shape["dom"], mesh.shape["sub"])
    wide = P(None, ("dom", "sub"))
    flat = P(("dom", "sub"))
    in_specs = (wide, wide, flat, wide, wide, wide, wide, wide, flat, flat)
    return jax.shard_map(
        functools.partial(body, sizes),
        mesh=mesh,
        in_specs=in_specs,
        out_specs=wide,
        check_vma=False,
    )
```

time: 85 us -> 15.1 us (0.18)
  the two profiles are of different devices: /device:TPU:26 before, /device:TPU:0 now
where the time goes in v1:
time: 15.1 us; the launch traced here: 15 us
  Pallas kernels  13.1 us (87%)
  local copies, waits for them, and re-layouts  1.87 us (12%)
    pallas_call x1, Pallas kernels, body(): pl.pallas_call(functools.partial(kernel, sizes), out_shape=jax.ShapeDtype...  13.1 us
    unnamed x1, local copies, waits for them, and re-layouts  1.87 us

profile of v1, /device:TPU:0, one launch (start us, length us, event | category | flops | bytes accessed | tf_op | source)
XLA Modules:
  0.0 15.0 jit_solution(9493359418286939115)
XLA Ops:
  0.0 13.1 %shard_map.118 = f32[512,256]{1,0:T(8,128)} custom-call(f32[512,256]{1,0:T(8,128)} %u_hbm.1, f32[512,256]{1,0:T(8,128)} %kappa_hbm.1, s32[1,256]{1,0:T(1,128)} %bitcast.2, s32[2,64]{1,0:T(2,128)} %local_hbm.1, s32[2,32]{1,0:T(2,128)} %sub_hbm.1, s32[2,32]{1,0:T(2,128)} %near_hbm.1, s32[2,12]{1,0:T(2,128)} %far_hbm.1, s32[4,3]{1,0:T(4,128)} %child_hbm.1, ...), custom_call_target="tpu_custom_call" | custom-call | tf_op jit(solution)/shard_map/pallas_call | solution.py:497
  13.1 1.9 %copy.14 = f32[512,256]{1,0:T(8,128)} copy(f32[512,256]{1,0:T(8,128)} %shard_map.118) | data formatting | bytes 1048576

commit v2 on v1

--- a/solution.py
+++ b/solution.py
@@ -113,10 +113,10 @@
     return jnp.where(inside, col, -1.0)
 
 
-def hot_rows(columns, base, elems):
+def hot_rows(columns, base, elems, kind=BF16):
     col = columns[0] if len(columns) == 1 else jnp.concatenate(columns, axis=0)
     lane = lax.broadcasted_iota(I32, (col.shape[0], elems), 1).astype(F32)
-    return jnp.where(lane == col - float(base), 1.0, 0.0).astype(BF16)
+    return jnp.where(lane == col - float(base), 1.0, 0.0).astype(kind)
 
 
 def line(values, matrix):
@@ -136,10 +136,11 @@
     return out
 
 
-def stencil(matrix):
-    big = np.kron(np.eye(16), matrix)
-    high, low = numpy_halves(big)
-    return np.concatenate([high, high], axis=1), low
+def stencils():
+    forth, back = np.kron(np.eye(16), DERIV), np.kron(np.eye(16), DERIV.T)
+    ends = np.concatenate([back[0::NPTS], back[NPTS - 1 :: NPTS]], axis=0)
+    pieces = [piece for table in (forth, back, ends) for piece in numpy_halves(table)]
+    return np.concatenate(pieces, axis=0)
 
 
 def kernel(
@@ -156,7 +157,7 @@
     deriv_hbm,
     mortar_hbm,
     peer_ref,
-    out_hbm,
+    out_ref,
     level_ref,
     local_ref,
     sub_ref,
@@ -170,6 +171,7 @@
     u_ref,
     k_ref,
     g_ref,
+    y_ref,
     side_out,
     side_in,
     msg_out,
@@ -202,18 +204,24 @@
             ]
         )
     ]
-    for copy in small[:7]:
-        copy.start()
-
-    def load(n, source, target, slot):
-        block = source.at[:, pl.ds(n * 128, 128)]
-        return pltpu.make_async_copy(block, target.at[n], load_sem.at[slot, n])
-
-    for n in range(parts):
-        load(n, u_hbm, u_ref, 0).start()
-        load(n, kappa_hbm, k_ref, 1).start()
-    for copy in small[7:]:
-        copy.start()
+    block = 128
+    blocks = NPTS**3 // block
+
+    def load(n, part, source, target, slot):
+        own = pl.ds(part * block, block)
+        return pltpu.make_async_copy(
+            source.at[own, pl.ds(n * 128, 128)], target.at[n, own], load_sem.at[slot, n, part]
+        )
+
+    small[7].start()
+    for part in range(blocks):
+        for n in range(parts):
+            load(n, part, u_hbm, u_ref, 0).start()
+            load(n, part, kappa_hbm, k_ref, 1).start()
+        if part == 0:
+            for copy in small[:7]:
+                copy.start()
+    small[8].start()
 
     barrier = pltpu.get_barrier_semaphore()
 
@@ -256,10 +264,11 @@
     hot2 = hot_rows([column(near_ref[0:1], up(near))], 2 * elems, elems)
     hot3 = hot_rows([column(near_ref[1:2], up(near))], 3 * elems, elems)
     children = [column(child_ref[m : m + 1], groupp) for m in range(4)]
-    hot4 = hot_rows([column(far_ref[0:1], farp)] + children, 4 * elems, elems)
-    hot5 = hot_rows(
-        [column(far_ref[1:2], farp), column(coarse_ref[...], coarsep)], 5 * elems, elems
+    hot4f = hot_rows([column(far_ref[0:1], farp)] + children, 4 * elems, elems, F32)
+    hot5f = hot_rows(
+        [column(far_ref[1:2], farp), column(coarse_ref[...], coarsep)], 5 * elems, elems, F32
     )
+    hot4, hot5, hot_kids = hot4f.astype(BF16), hot5f.astype(BF16), hot4f[farp:].astype(BF16)
 
     sources = 2 * farp + groupp + coarsep
     rows = 8 * n_dom
@@ -281,12 +290,9 @@
     def hot(mask):
         return jnp.where(mask, 1.0, 0.0).astype(BF16)
 
-    route = hot(
-        lax.broadcasted_iota(I32, (rows, sources), 0) == keys((1, sources), 1, 4, 5)
-    )
-    unroute = hot(
-        lax.broadcasted_iota(I32, (sources, rows), 1) == keys((sources, 1), 0, 5, 4)
-    )
+    row = lax.broadcasted_iota(I32, (rows, sources), 0)
+    route = hot(row == keys((1, sources), 1, 4, 5))
+    origin = hot(row == keys((1, sources), 1, 5, 4))
 
     scale = jnp.exp2(-level_ref[...].astype(F32))
     sub8 = lax.broadcasted_iota(I32, (8, elems), 0)
@@ -305,49 +311,52 @@
         for n in range(parts):
             w_ref[n, own, :] += values[:, n * 128 : (n + 1) * 128]
 
-    for n in range(parts):
-        load(n, u_hbm, u_ref, 0).wait()
-        load(n, kappa_hbm, k_ref, 1).wait()
-        here = weight[:, n * 128 : (n + 1) * 128]
-        for j in range(NPTS):
-            flux = line([u_ref[n, slab(i, j), :] for i in range(NPTS)], DERIV)
-            for i in range(NPTS):
-                g = k_ref[n, slab(i, j), :] * (here * float(WEIGHTS[i] * WEIGHTS[j]))
-                g_ref[n, slab(i, j), :] = g
-                flux[i] = flux[i] * g
-            flux = line(flux, DERIV.T)
-            for i in range(NPTS):
-                w_ref[n, slab(i, j), :] = flux[i]
-        for i in range(NPTS):
-            flux = line([u_ref[n, slab(i, j), :] for j in range(NPTS)], DERIV)
-            flux = [flux[j] * g_ref[n, slab(i, j), :] for j in range(NPTS)]
-            flux = line(flux, DERIV.T)
-            for j in range(NPTS):
-                w_ref[n, slab(i, j), :] += flux[j]
-    for copy in small[7:]:
-        copy.wait()
-    block = 128
-    for part in range(NPTS**3 // block):
+    small[7].wait()
+    turns = [deriv_ref[128 * n : 128 * n + 128, :] for n in range(4)]
+    ends = [deriv_ref[512 + 32 * n : 544 + 32 * n, :] for n in range(2)]
+
+    def along(pair, values):
+        high, low = halves_of(values)
+        both = jnp.concatenate([high, low], axis=0)
+        return dot(jnp.concatenate([pair[0], pair[0]], axis=1), both) + dot(pair[1], high)
+
+    low_face, high_face = [], []
+    for part in range(blocks):
         own = pl.ds(part * block, block)
-        high, low = halves_of(across(u_ref, own))
-        flux = dot(deriv_ref[0:block, 0 : 2 * block], jnp.concatenate([high, low], axis=0))
-        flux += dot(deriv_ref[0:block, 2 * block : 3 * block], high)
-        high, low = halves_of(flux * across(g_ref, own))
-        turn = dot(deriv_ref[block : 2 * block, 0 : 2 * block], jnp.concatenate([high, low], axis=0))
-        turn += dot(deriv_ref[block : 2 * block, 2 * block : 3 * block], high)
-        add_across(own, turn)
+        for n in range(parts):
+            load(n, part, u_hbm, u_ref, 0).wait()
+            load(n, part, kappa_hbm, k_ref, 1).wait()
+        for n in range(parts):
+            here = weight[:, n * 128 : (n + 1) * 128]
+            for i in range(part * 2, part * 2 + 2):
+                for j in range(NPTS):
+                    g_ref[n, slab(i, j), :] = k_ref[n, slab(i, j), :] * (
+                        here * float(WEIGHTS[i] * WEIGHTS[j])
+                    )
+        flux = along(turns[0:2], across(u_ref, own)) * across(g_ref, own)
+        for n in range(parts):
+            y_ref[n, own, :] = flux[:, n * 128 : (n + 1) * 128]
+        end = along(ends, flux)
+        low_face.append(end[0:16])
+        high_face.append(end[16:32])
 
     square = NPTS * NPTS
     last = NPTS - 1
     low_i, high_i = pl.ds(0, square), pl.ds(last * square, square)
     low_k, high_k = pl.ds(0, square, NPTS), pl.ds(last, square, NPTS)
-    face0 = across(w_ref, low_i)
-    face1 = across(w_ref, high_i)
-    face2 = jnp.concatenate([across(w_ref, slab(i, 0)) for i in range(NPTS)], axis=0)
-    face3 = jnp.concatenate([across(w_ref, slab(i, last)) for i in range(NPTS)], axis=0)
-    face4 = across(w_ref, low_k)
-    face5 = across(w_ref, high_k)
-
+    u4, u5, g4, g5 = (across(r, k) for r in (u_ref, g_ref) for k in (low_k, high_k))
+    flux = along(turns[0:2], jnp.concatenate([u4, u5], axis=0))
+    flux = along(turns[2:4], flux * jnp.concatenate([g4, g5], axis=0))
+
+    def across_i(u, g):
+        part = line([u[i * NPTS : (i + 1) * NPTS] for i in range(NPTS)], DERIV)
+        part = [part[i] * g[i * NPTS : (i + 1) * NPTS] for i in range(NPTS)]
+        return jnp.concatenate(line(part, DERIV.T), axis=0)
+
+    face4 = jnp.concatenate(low_face, axis=0) + flux[0:square] + across_i(u4, g4)
+    face5 = jnp.concatenate(high_face, axis=0) + flux[square:] + across_i(u5, g5)
+
+    small[8].wait()
     taken4 = take_rows(hot4, face4)
     taken5 = take_rows(hot5, face5)
     family = [taken4[farp + m * groupp : farp + (m + 1) * groupp] for m in range(4)]
@@ -360,11 +369,6 @@
     message = select(route, source)
     for p in range(n_dom):
         msg_out[p, :, 0:square] = message[8 * p : 8 * p + 8]
-    side_out[0, 0:rim, 0:square] = take_rows(hot0s, face0)[0:rim]
-    side_out[1, 0:rim, 0:square] = take_rows(hot1s, face1)[0:rim]
-    side_out[2, 0:near, 0:square] = take_rows(hot2, face2)[0:near]
-    side_out[3, 0:near, 0:square] = take_rows(hot3, face3)[0:near]
-
     pl.semaphore_wait(
         barrier, n_dom - 1 + (sub > 0).astype(I32) + (sub < n_sub - 1).astype(I32)
     )
@@ -413,10 +417,62 @@
         return carry
 
     lax.fori_loop(1, n_dom, start_all, 0, unroll=n_dom <= 8)
+
+    for part in range(blocks):
+        own = pl.ds(part * block, block)
+        turn = along(turns[2:4], across(y_ref, own))
+        for n in range(parts):
+            w_ref[n, own, :] = turn[:, n * 128 : (n + 1) * 128]
+    for n in range(parts):
+        for j in range(NPTS):
+            flux = line([u_ref[n, slab(i, j), :] for i in range(NPTS)], DERIV)
+            flux = [flux[i] * g_ref[n, slab(i, j), :] for i in range(NPTS)]
+            flux = line(flux, DERIV.T)
+            for i in range(NPTS):
+                w_ref[n, slab(i, j), :] += flux[i]
+        for i in range(NPTS):
+            flux = line([u_ref[n, slab(i, j), :] for j in range(NPTS)], DERIV)
+            flux = [flux[j] * g_ref[n, slab(i, j), :] for j in range(NPTS)]
+            flux = line(flux, DERIV.T)
+            for j in range(NPTS):
+                w_ref[n, slab(i, j), :] += flux[j]
+    face0 = across(w_ref, low_i)
+    face1 = across(w_ref, high_i)
+    face2 = jnp.concatenate([across(w_ref, slab(i, 0)) for i in range(NPTS)], axis=0)
+    face3 = jnp.concatenate([across(w_ref, slab(i, last)) for i in range(NPTS)], axis=0)
+    side_out[0, 0:rim, 0:square] = take_rows(hot0s, face0)[0:rim]
+    side_out[1, 0:rim, 0:square] = take_rows(hot1s, face1)[0:rim]
+    side_out[2, 0:near, 0:square] = take_rows(hot2, face2)[0:near]
+    side_out[3, 0:near, 0:square] = take_rows(hot3, face3)[0:near]
+
     for there, mine, theirs, device in sides:
         @pl.when(there)
         def _():
             side_copy(mine, theirs, device).start()
+
+    share = [product(projected, lift[m]) - family[m] for m in range(4)]
+    add_across(low_k, spread_rows(jnp.concatenate(share, axis=0), hot_kids))
+
+    def rows_at(first, values):
+        pieces = []
+        if first:
+            pieces.append(jnp.zeros((first, elems), F32))
+        pieces.append(values)
+        if first + values.shape[0] < sources:
+            pieces.append(jnp.zeros((sources - first - values.shape[0], elems), F32))
+        return pieces[0] if len(pieces) == 1 else jnp.concatenate(pieces, axis=0)
+
+    def land(values):
+        return dot(origin, values.astype(BF16)).astype(BF16)
+
+    land4 = land(rows_at(0, hot4f[0:farp]))
+    land5 = land(rows_at(farp, hot5f[0:farp]) + rows_at(2 * farp + groupp, hot5f[farp:]))
+    first = farp
+    land_kids = []
+    for m in range(4):
+        land_kids.append(land(rows_at(2 * farp, hot4f[first : first + groupp])))
+        first += groupp
+    kron = halves_of(mortar_ref[:, 0:square])
 
     add_across(low_i, spread_rows(take_rows(hot1l, face1), hot0l))
     add_across(high_i, spread_rows(take_rows(hot0l, face0), hot1l))
@@ -440,21 +496,17 @@
 
     lax.fori_loop(1, n_dom, wait_all, 0, unroll=n_dom <= 8)
     received = jnp.concatenate([msg_in[p, :, 0:square] for p in range(n_dom)], axis=0)
-    back = select(unroute, received)
-    summed = back[2 * farp : 2 * farp + groupp] + projected
-    add4 = [back[0:farp]] + [product(summed, lift[m]) - family[m] for m in range(4)]
-    add5 = [back[farp : 2 * farp], back[2 * farp + groupp :]]
-    add_across(low_k, spread_rows(jnp.concatenate(add4, axis=0), hot4))
-    add_across(high_k, spread_rows(jnp.concatenate(add5, axis=0), hot5))
-
-    def store(n):
-        block = out_hbm.at[:, pl.ds(n * 128, 128)]
-        return pltpu.make_async_copy(w_ref.at[n], block, load_sem.at[0, n])
-
+    high, low = halves_of(received.T)
+    add5 = dot(high, land5) + dot(low, land5)
+    add4 = dot(high, land4) + dot(low, land4)
+    lifted = dot(kron[0], high) + dot(kron[0], low) + dot(kron[1], high)
+    for m in range(4):
+        high, low = halves_of(lifted[m * square : (m + 1) * square])
+        add4 += dot(high, land_kids[m]) + dot(low, land_kids[m])
+    add_across(high_k, add5)
+    add_across(low_k, add4)
     for n in range(parts):
-        store(n).start()
-    for n in range(parts):
-        store(n).wait()
+        out_ref[:, n * 128 : (n + 1) * 128] = w_ref[n]
 
 
 def body(
@@ -472,11 +524,6 @@
 ):
     n_dom, n_sub = sizes
     elems = nodal_values.shape[1]
-    double, single = stencil(DERIV)
-    double_t, single_t = stencil(DERIV.T)
-    deriv = np.concatenate(
-        [np.concatenate([double, single], 1), np.concatenate([double_t, single_t], 1)], 0
-    )
     krons = [np.kron(HALVES[m // 2], HALVES[m % 2]) for m in range(4)]
     mortar = np.concatenate([np.concatenate([m, m.T], axis=1) for m in krons], axis=0)
     held = (elems // 128, NPTS**3, 128)
@@ -489,18 +536,20 @@
         far_faces,
         child_faces,
         coarse_faces.reshape(1, n_dom),
-        jnp.asarray(deriv, BF16),
+        jnp.asarray(stencils(), BF16),
         jnp.asarray(mortar, F32),
     ]
     smem = pl.BlockSpec(memory_space=pltpu.SMEM)
-    hbm = pl.BlockSpec(memory_space=pl.ANY)
+    hbm = pl.BlockSpec(memory_space=pltpu.HBM)
+    vmem = pl.BlockSpec(memory_space=pltpu.VMEM)
     return pl.pallas_call(
         functools.partial(kernel, sizes),
-        out_shape=jax.ShapeDtypeStruct(nodal_values.shape, F32),
+        out_shape=pltpu.VMEM(nodal_values.shape, F32),
         in_specs=[hbm] * 11 + [smem],
-        out_specs=hbm,
+        out_specs=vmem,
         scratch_shapes=[pltpu.VMEM(item.shape, item.dtype) for item in small]
         + [
+            pltpu.VMEM(held, F32),
             pltpu.VMEM(held, F32),
             pltpu.VMEM(held, F32),
             pltpu.VMEM(held, F32),
@@ -510,7 +559,7 @@
             pltpu.VMEM((n_dom, 8, 128), F32),
             pltpu.VMEM((n_dom, 8, 128), F32),
             pltpu.SemaphoreType.DMA((len(small),)),
-            pltpu.SemaphoreType.DMA((2, held[0])),
+            pltpu.SemaphoreType.DMA((2, held[0], NPTS**3 // 128)),
             pltpu.SemaphoreType.DMA((4,)),
             pltpu.SemaphoreType.DMA((4,)),
             pltpu.SemaphoreType.DMA((n_dom,)),

time: 15.1 us -> 13.8 us (0.914)
  local copies, waits for them, and re-layouts: 1.87 us -> 0.8 us
  Pallas kernels: 13.1 us -> 12.8 us
    unnamed x1, local copies, waits for them, and re-layouts: 1.87 us -> 0.8 us
    pallas_call x1, Pallas kernels: 13.1 us -> 12.8 us  [body(): pl.pallas_call(functools.partial(kernel, sizes), out_shape=pltpu.VMEM(nod...]
where the time goes in v2:
time: 13.8 us; the launch traced here: 13.6 us
  Pallas kernels  12.8 us (93%)
  local copies, waits for them, and re-layouts  0.8 us (6%)
    pallas_call x1, Pallas kernels, body(): pl.pallas_call(functools.partial(kernel, sizes), out_shape=pltpu.VMEM(nod...  12.8 us
    unnamed x1, local copies, waits for them, and re-layouts  0.8 us

profile of v2, /device:TPU:0, one launch (start us, length us, event | category | flops | bytes accessed | tf_op | source)
XLA Modules:
  0.0 13.6 jit_solution(8127490528042537677)
XLA Ops:
  0.0 12.8 %shard_map.118 = f32[512,256]{1,0:T(8,128)S(1)} custom-call(f32[512,256]{1,0:T(8,128)} %u_hbm.1, f32[512,256]{1,0:T(8,128)} %kappa_hbm.1, s32[1,256]{1,0:T(1,128)} %bitcast.2, s32[2,64]{1,0:T(2,128)} %local_hbm.1, s32[2,32]{1,0:T(2,128)} %sub_hbm.1, s32[2,32]{1,0:T(2,128)} %near_hbm.1, s32[2,12]{1,0:T(2,128)} %far_hbm.1, s32[4,3]{1,0:T(4,128)} %child_hbm.1, ...), custom_call_target="tpu_custom_call" | custom-call | tf_op jit(solution)/shard_map/pallas_call | solution.py:545
  12.8 0.8 %copy.14 = f32[512,256]{1,0:T(8,128)} copy(f32[512,256]{1,0:T(8,128)S(1)} %shard_map.118) | data formatting | bytes 1048576

commit v3 on v2

--- a/solution.py
+++ b/solution.py
@@ -156,7 +156,7 @@
     coarse_hbm,
     deriv_hbm,
     mortar_hbm,
-    peer_ref,
+    peer_hbm,
     out_ref,
     level_ref,
     local_ref,
@@ -167,6 +167,7 @@
     coarse_ref,
     deriv_ref,
     mortar_ref,
+    peer_ref,
     w_ref,
     u_ref,
     k_ref,
@@ -201,6 +202,7 @@
                 (level_hbm, level_ref),
                 (deriv_hbm, deriv_ref),
                 (mortar_hbm, mortar_ref),
+                (peer_hbm, peer_ref),
             ]
         )
     ]
@@ -213,14 +215,13 @@
             source.at[own, pl.ds(n * 128, 128)], target.at[n, own], load_sem.at[slot, n, part]
         )
 
+    for copy in small[:7] + small[9:]:
+        copy.start()
     small[7].start()
     for part in range(blocks):
         for n in range(parts):
             load(n, part, u_hbm, u_ref, 0).start()
             load(n, part, kappa_hbm, k_ref, 1).start()
-        if part == 0:
-            for copy in small[:7]:
-                copy.start()
     small[8].start()
 
     barrier = pltpu.get_barrier_semaphore()
@@ -251,7 +252,7 @@
     clear(me == n_dom - 1, 3)
     msg_in[me] = jnp.zeros(msg_in.shape[1:], F32)
 
-    for copy in small[:7]:
+    for copy in small[:7] + small[9:]:
         copy.wait()
 
     pairs, rim, near = local_ref.shape[1], sub_ref.shape[1], near_ref.shape[1]
@@ -294,6 +295,32 @@
     route = hot(row == keys((1, sources), 1, 4, 5))
     origin = hot(row == keys((1, sources), 1, 5, 4))
 
+    def rows_at(first, values):
+        pieces = []
+        if first:
+            pieces.append(jnp.zeros((first, elems), F32))
+        pieces.append(values)
+        if first + values.shape[0] < sources:
+            pieces.append(jnp.zeros((sources - first - values.shape[0], elems), F32))
+        return pieces[0] if len(pieces) == 1 else jnp.concatenate(pieces, axis=0)
+
+    def land(where, values):
+        return dot(where, values.astype(BF16)).astype(BF16)
+
+    at_five = rows_at(farp, hot5f[0:farp]) + rows_at(2 * farp + groupp, hot5f[farp:])
+    send5 = land(route, at_five)
+    send4 = [dot(route, rows_at(0, hot4f[0:farp]).astype(BF16))]
+    dom_row = lax.broadcasted_iota(I32, (n_dom, groupp), 0)
+    dom_slot = lax.broadcasted_iota(I32, (n_dom, groupp), 1)
+    named = jnp.full((n_dom, groupp), -1, I32)
+    for slot in range(groups):
+        named = jnp.where(dom_slot == slot, peer_ref[slot], named)
+    named = hot(named == dom_row)
+    for m in range(4):
+        first = farp + m * groupp
+        send4.append(dot(named, hot4f[first : first + groupp].astype(BF16)))
+    send4 = jnp.concatenate(send4, axis=0).astype(BF16)
+
     scale = jnp.exp2(-level_ref[...].astype(F32))
     sub8 = lax.broadcasted_iota(I32, (8, elems), 0)
     weight = jnp.zeros((8, elems), F32)
@@ -323,9 +350,12 @@
     low_face, high_face = [], []
     for part in range(blocks):
         own = pl.ds(part * block, block)
-        for n in range(parts):
-            load(n, part, u_hbm, u_ref, 0).wait()
-            load(n, part, kappa_hbm, k_ref, 1).wait()
+        if part == 0:
+            for n in range(blocks * parts):
+                load(n // blocks, n % blocks, u_hbm, u_ref, 0).wait()
+                load(n // blocks, n % blocks, kappa_hbm, k_ref, 1).wait()
+        if part == 0:
+            small[8].wait()
         for n in range(parts):
             here = weight[:, n * 128 : (n + 1) * 128]
             for i in range(part * 2, part * 2 + 2):
@@ -356,19 +386,17 @@
     face4 = jnp.concatenate(low_face, axis=0) + flux[0:square] + across_i(u4, g4)
     face5 = jnp.concatenate(high_face, axis=0) + flux[square:] + across_i(u5, g5)
 
-    small[8].wait()
-    taken4 = take_rows(hot4, face4)
-    taken5 = take_rows(hot5, face5)
-    family = [taken4[farp + m * groupp : farp + (m + 1) * groupp] for m in range(4)]
     down = [mortar_ref[m * square : (m + 1) * square, 0:square] for m in range(4)]
     lift = [mortar_ref[m * square : (m + 1) * square, square:] for m in range(4)]
-    projected = sum(product(family[m], down[m]) for m in range(4))
-    source = jnp.concatenate(
-        [taken4[0:farp], taken5[0:farp], projected, taken5[farp:]], axis=0
-    )
-    message = select(route, source)
+    message = take_rows(send5, face5)
+    taken4 = take_rows(send4, face4)
+    message += taken4[0:rows]
+    kids = [taken4[rows + m * n_dom : rows + (m + 1) * n_dom] for m in range(4)]
+    sent = sum(product(kids[m], down[m]) for m in range(4))
     for p in range(n_dom):
         msg_out[p, :, 0:square] = message[8 * p : 8 * p + 8]
+        msg_out[p, 4:5, 0:square] = sent[p : p + 1]
+
     pl.semaphore_wait(
         barrier, n_dom - 1 + (sub > 0).astype(I32) + (sub < n_sub - 1).astype(I32)
     )
@@ -450,28 +478,21 @@
         def _():
             side_copy(mine, theirs, device).start()
 
-    share = [product(projected, lift[m]) - family[m] for m in range(4)]
-    add_across(low_k, spread_rows(jnp.concatenate(share, axis=0), hot_kids))
-
-    def rows_at(first, values):
-        pieces = []
-        if first:
-            pieces.append(jnp.zeros((first, elems), F32))
-        pieces.append(values)
-        if first + values.shape[0] < sources:
-            pieces.append(jnp.zeros((sources - first - values.shape[0], elems), F32))
-        return pieces[0] if len(pieces) == 1 else jnp.concatenate(pieces, axis=0)
-
-    def land(values):
-        return dot(origin, values.astype(BF16)).astype(BF16)
-
-    land4 = land(rows_at(0, hot4f[0:farp]))
-    land5 = land(rows_at(farp, hot5f[0:farp]) + rows_at(2 * farp + groupp, hot5f[farp:]))
+    taken4 = take_rows(hot_kids, face4)
+    family = [taken4[m * groupp : (m + 1) * groupp] for m in range(4)]
+    projected = sum(product(family[m], down[m]) for m in range(4))
+
+    land4 = land(origin, rows_at(0, hot4f[0:farp]))
+    land5 = land(origin, at_five)
     first = farp
     land_kids = []
     for m in range(4):
-        land_kids.append(land(rows_at(2 * farp, hot4f[first : first + groupp])))
+        land_kids.append(land(origin, rows_at(2 * farp, hot4f[first : first + groupp])))
         first += groupp
+
+    share = [product(projected, lift[m]) - family[m] for m in range(4)]
+    add_across(low_k, spread_rows(jnp.concatenate(share, axis=0), hot_kids))
+
     kron = halves_of(mortar_ref[:, 0:square])
 
     add_across(low_i, spread_rows(take_rows(hot1l, face1), hot0l))
@@ -539,16 +560,16 @@
         jnp.asarray(stencils(), BF16),
         jnp.asarray(mortar, F32),
     ]
-    smem = pl.BlockSpec(memory_space=pltpu.SMEM)
     hbm = pl.BlockSpec(memory_space=pltpu.HBM)
     vmem = pl.BlockSpec(memory_space=pltpu.VMEM)
     return pl.pallas_call(
         functools.partial(kernel, sizes),
         out_shape=pltpu.VMEM(nodal_values.shape, F32),
-        in_specs=[hbm] * 11 + [smem],
+        in_specs=[hbm] * 12,
         out_specs=vmem,
         scratch_shapes=[pltpu.VMEM(item.shape, item.dtype) for item in small]
         + [
+            pltpu.SMEM(child_peer.shape, I32),
             pltpu.VMEM(held, F32),
             pltpu.VMEM(held, F32),
             pltpu.VMEM(held, F32),
@@ -558,7 +579,7 @@
             pltpu.VMEM((4, side_rows, 128), F32),
             pltpu.VMEM((n_dom, 8, 128), F32),
             pltpu.VMEM((n_dom, 8, 128), F32),
-            pltpu.SemaphoreType.DMA((len(small),)),
+            pltpu.SemaphoreType.DMA((len(small) + 1,)),
             pltpu.SemaphoreType.DMA((2, held[0], NPTS**3 // 128)),
             pltpu.SemaphoreType.DMA((4,)),
             pltpu.SemaphoreType.DMA((4,)),

time: 13.8 us -> 12.8 us (0.928)
  Pallas kernels: 12.8 us -> 11.9 us
    pallas_call x1, Pallas kernels: 12.8 us -> 11.9 us  [body(): pl.pallas_call(functools.partial(kernel, sizes), out_shape=pltpu.VMEM(nod...]
where the time goes in v3:
time: 12.8 us; the launch traced here: 12.7 us
  Pallas kernels  11.9 us (93%)
  local copies, waits for them, and re-layouts  0.8 us (6%)
    pallas_call x1, Pallas kernels, body(): pl.pallas_call(functools.partial(kernel, sizes), out_shape=pltpu.VMEM(nod...  11.9 us
    unnamed x1, local copies, waits for them, and re-layouts  0.8 us

profile of v3, /device:TPU:0, one launch (start us, length us, event | category | flops | bytes accessed | tf_op | source)
XLA Modules:
  0.0 12.7 jit_solution(3558205820539622781)
XLA Ops:
  0.0 11.9 %shard_map.118 = f32[512,256]{1,0:T(8,128)S(1)} custom-call(f32[512,256]{1,0:T(8,128)} %u_hbm.1, f32[512,256]{1,0:T(8,128)} %kappa_hbm.1, s32[1,256]{1,0:T(1,128)} %bitcast.2, s32[2,64]{1,0:T(2,128)} %local_hbm.1, s32[2,32]{1,0:T(2,128)} %sub_hbm.1, s32[2,32]{1,0:T(2,128)} %near_hbm.1, s32[2,12]{1,0:T(2,128)} %far_hbm.1, s32[4,3]{1,0:T(4,128)} %child_hbm.1, ...), custom_call_target="tpu_custom_call" | custom-call | tf_op jit(solution)/shard_map/pallas_call | solution.py:565
  11.9 0.8 %copy.14 = f32[512,256]{1,0:T(8,128)} copy(f32[512,256]{1,0:T(8,128)S(1)} %shard_map.118) | data formatting | bytes 1048576
